TPU v7x, 32 devices: a whole 2x2x4 slice. The times are simulated.
32 devices in a mesh: dp: 4 (over x, core), context: 8 (over z, y).
Axes of the slice: x: 2, y: 2, z: 4, core: 2. Of those that a mesh axis runs over, the one named last changes fastest.
Arguments:
- signal: bfloat16 [8192, 2048], P('context', 'dp'), may hold values from -6 to 6
- gating: bfloat16 [8192, 2048], P('context', 'dp'), may hold values from -6 to 6
- writer: bfloat16 [8192, 128], P('context'), may hold values from -2 to 2
- reader: bfloat16 [8192, 128], P('context'), may hold values from -2 to 2
- step_raw: float32 [8192, 32], P('context', 'dp'), may hold values from -7 to -1
- decay_log: float32 [32], P('dp'), may hold values from -12 to 1
- skip_gain: float32 [32], P('dp'), may hold values from 0.5 to 2
- norm_gain: float32 [2048], P('dp'), may hold values from 0.25 to 1.75
- cotangent: bfloat16 [8192, 2048], P('context', 'dp'), may hold values from -6 to 6
Outputs:
- grad_signal: bfloat16 [8192, 2048], P('context', 'dp')
- grad_gating: bfloat16 [8192, 2048], P('context', 'dp')
- grad_bc: float32 [8192, 256], P('context', 'dp')
- grad_step: float32 [8192, 32], P('context', 'dp')
All inputs are finite; a program needn't handle non-finite values.
Results may differ from a plain program's by a relative error of at most 0.0011.
Values sent between devices are 32-bit elements; how exact they have to be, the bound alone decides.
No kernel may reach another device: no remote copies, remote signals or barrier semaphores. Data moves between devices by JAX's collectives and lax.ppermute only.
A program may use at most 64 MiB of HBM per device.

v0:
```python
from functools import partial
import jax
import jax.numpy as jnp
from jax import lax
from jax.sharding import PartitionSpec as P

HEADS = 32
HEAD_DIM = 64
SPAN = 256
highest = lax.Precision.HIGHEST
epsilon = 1e-05


def block_step(state, pieces, decay_rate, skip_gain):
    signal_block, writer_block, reader_block, raw_block = pieces
    step_size = jax.nn.softplus(raw_block)
    log_decay = step_size * decay_rate[None, :]
    running = jnp.cumsum(log_decay, axis=0)
    length = raw_block.shape[0]
    causal = jnp.arange(length)[:, None] >= jnp.arange(length)[None, :]
    log_gaps = running[:, None, :] - running[None, :, :]
    decays = jnp.exp(jnp.where(causal[:, :, None], log_gaps, -jnp.inf))
    scores = jnp.dot(
        reader_block, writer_block.T, precision=highest, preferred_element_type=jnp.float32
    )
    mixing = scores[:, :, None] * decays * step_size[None, :, :]
    within = jnp.einsum("tsh,shp->thp", mixing, signal_block, precision=highest)
    across = jnp.exp(running)[:, :, None] * jnp.einsum(
        "tn,hpn->thp", reader_block, state, precision=highest
    )
    result = within + across + skip_gain[None, :, None] * signal_block
    weights = jnp.exp(running[-1][None, :] - running) * step_size
    new_state = jnp.exp(running[-1])[:, None, None] * state + jnp.einsum(
        "sh,shp,sn->hpn", weights, signal_block, writer_block, precision=highest
    )
    return (new_state, result)


def recurrence(signal, writer, reader, step_raw, start_state, decay_rate, skip_gain):
    tokens, head_count = step_raw.shape
    blocks = tokens // SPAN
    pieces = (
        signal.reshape(blocks, SPAN, head_count, HEAD_DIM),
        writer.reshape(blocks, SPAN, -1),
        reader.reshape(blocks, SPAN, -1),
        step_raw.reshape(blocks, SPAN, head_count),
    )
    advance = jax.checkpoint(partial(block_step, decay_rate=decay_rate, skip_gain=skip_gain))
    end_state, outputs = lax.scan(advance, start_state, pieces)
    return (outputs.reshape(tokens, head_count * HEAD_DIM), end_state)


def on_device(signal, gating, writer, reader, step_raw, decay_log, skip_gain, norm_gain, cotangent):
    tokens, head_count = step_raw.shape
    decay_rate = -jnp.exp(decay_log)
    signal_f = signal.astype(jnp.float32)
    writer_f = writer.astype(jnp.float32)
    reader_f = reader.astype(jnp.float32)
    step_size = jax.nn.softplus(step_raw)
    running = jnp.cumsum(step_size * decay_rate[None, :], axis=0)
    totals = running[-1]
    weights = jnp.exp(totals[None, :] - running) * step_size
    local_end = jnp.einsum(
        "sh,shp,sn->hpn",
        weights,
        signal_f.reshape(tokens, head_count, HEAD_DIM),
        writer_f,
        precision=highest,
    )
    all_totals = lax.all_gather(totals[None, :], "context", axis=0, tiled=True)
    inclusive = jnp.cumsum(all_totals, axis=0)
    exclusive = inclusive - all_totals
    position = lax.axis_index("context")
    devices = all_totals.shape[0]
    mine = (jnp.arange(devices) == position).astype(jnp.float32)
    inclusive_mine = jnp.dot(mine, inclusive, precision=highest, preferred_element_type=jnp.float32)
    exclusive_mine = jnp.dot(mine, exclusive, precision=highest, preferred_element_type=jnp.float32)
    pieces = lax.all_gather(local_end[None], "context", axis=0, tiled=True)
    indices = jnp.arange(pieces.shape[0])
    select = (indices[:, None] == jnp.arange(devices)[None, :]).astype(jnp.float32)
    inclusive_from = jnp.dot(
        select, inclusive, precision=highest, preferred_element_type=jnp.float32
    )
    factors = jnp.where(
        (indices < position)[:, None],
        jnp.exp(jnp.minimum(exclusive_mine[None, :] - inclusive_from, 0.0)),
        0.0,
    )
    incoming = jnp.einsum("fh,fhpn->hpn", factors, pieces, precision=highest)

    def local_pass(signal_in, writer_in, reader_in, raw_in, state_in):
        return recurrence(signal_in, writer_in, reader_in, raw_in, state_in, decay_rate, skip_gain)

    primal_out, pullback = jax.vjp(local_pass, signal_f, writer_f, reader_f, step_raw, incoming)
    output = primal_out[0]
    gating_f = gating.astype(jnp.float32)
    cotangent_f = cotangent.astype(jnp.float32)
    sigmoid = jax.nn.sigmoid(gating_f)
    activation = gating_f * sigmoid
    gated_output = output * activation
    weighted = norm_gain[None, :] * cotangent_f
    statistics = lax.psum(
        (jnp.sum(gated_output * gated_output, axis=1), jnp.sum(weighted * gated_output, axis=1)),
        "dp",
    )
    full_width = HEADS * HEAD_DIM
    scaling = lax.rsqrt(statistics[0] / full_width + epsilon)
    grad_gated = (
        weighted * scaling[:, None]
        - gated_output * (scaling * scaling * scaling * statistics[1] / full_width)[:, None]
    )
    grad_output = grad_gated * activation
    grad_gating = grad_gated * output * sigmoid * (1.0 + gating_f * (1.0 - sigmoid))
    influence = jnp.einsum(
        "th,thp,tn->hpn",
        jnp.exp(running),
        grad_output.reshape(tokens, head_count, HEAD_DIM),
        reader_f,
        precision=highest,
    )
    pieces = lax.all_gather(influence[None], "context", axis=0, tiled=True)
    indices = jnp.arange(pieces.shape[0])
    select = (indices[:, None] == jnp.arange(devices)[None, :]).astype(jnp.float32)
    exclusive_from = jnp.dot(
        select, exclusive, precision=highest, preferred_element_type=jnp.float32
    )
    factors = jnp.where(
        (indices > position)[:, None],
        jnp.exp(jnp.minimum(exclusive_from - inclusive_mine[None, :], 0.0)),
        0.0,
    )
    later_grad = jnp.einsum("fh,fhpn->hpn", factors, pieces, precision=highest)
    gradients = pullback((grad_output, later_grad))
    grad_signal = gradients[0]
    grad_writer = gradients[1]
    grad_reader = gradients[2]
    grad_step = gradients[3]
    grad_bc = lax.psum_scatter(
        jnp.concatenate([grad_writer, grad_reader], axis=1), "dp", scatter_dimension=1, tiled=True
    )
    return (grad_signal.astype(jnp.bfloat16), grad_gating.astype(jnp.bfloat16), grad_bc, grad_step)


def solution(mesh):
    in_specs = (
        P("context", "dp"),
        P("context", "dp"),
        P("context", None),
        P("context", None),
        P("context", "dp"),
        P("dp"),
        P("dp"),
        P("dp"),
        P("context", "dp"),
    )
    out_specs = (P("context", "dp"), P("context", "dp"), P("context", "dp"), P("context", "dp"))
    return jax.shard_map(
        on_device, mesh=mesh, in_specs=in_specs, out_specs=out_specs, check_vma=False
    )
```

profile of v0, /device:TPU:0, one launch (start us, length us, event | category | flops | bytes accessed | tf_op | source)
XLA Modules:
  0.0 398.9 jit_solution(4576556629796148414)
XLA Ops:
  18.4 22.6 %all-gather.2 = f32[8,1,8]{2,1,0:T(1,128)S(1)} all-gather(f32[1,1,8]{2,1,0:T(1,128)S(1)} %bitcast.366), channel_id=1, replica_groups=mesh['dp'=4,'context'=8] {'context'}, dimensions={0}, use_global_device_ids=true | all-gather | bytes 288 | tf_op jit(solution)/shard_map/all_gather | solution.py:70
  47.6 21.7 %all-gather.6.cloned.1.call-done = f32[64,64,128]{2,1,0:T(8,128)} async-done(((f32[8,64,128]{2,1,0:T(8,128)}), f32[64,64,128]{2,1,0:T(8,128)}) %all-gather.6.cloned.1.call-update) | async-done | bytes 2097168 | tf_op jit(solution)/shard_map/all_gather | solution.py:78
  69.4 4.4 %fusion.102 = f32[8,1,64,128]{3,1,2,0:T(1,128)S(1)} fusion(f32[8,8,1,1]{0,2,3,1:T(1,128)S(1)} %copy.85, f32[8,8,64,128]{3,2,1,0:T(8,128)} %bitcast.349), kind=kOutput, calls=%fused_computation.142 | convolution fusion | flops 6291456 | bytes 2359552 | tf_op jit(solution)/shard_map/fh,fhpn->hpn/dot_general | solution.py:89
  73.8 92.1 %while.39 = (s32[]{:T(128)}, f32[8,64,128]{2,1,0:T(8,128)S(1)}, f32[4,256,8,64]{1,0,3,2:T(4,128)}, f32[4,8,64,128]{3,2,1,0:T(8,128)}, f32[4,256,8]{1,2,0:T(8,128...) while((s32[]{:T(128)}, f32[8,64,128]{2,1,0:T(8,128)S(1)}, ...), condition=%wide.region_6.7_spmd.clone, body=%wide.region_3.6_spmd.clone.sunk | while | flops 909158400 | bytes 7812925 | solution.py:49
  76.1 3.5 fusion.231
  81.8 12.3 %dynamic_update_slice.68 = f32[4,256,8,64]{1,0,3,2:T(4,128)} dynamic-update-slice(f32[4,256,8,64]{1,0,3,2:T(4,128)} %get-tuple-element.828, f32[1,256,8,64]{1,0,3,2:T(1,128)S(1)} %copy.123, s32[]{:T(128)} %get-tuple-element.826, s32[]{:T(128)} %constant.134.clone.1..sunk, s32[]{:T(128)} %constant.134.clone.1..sunk, s32[]{:T(128)} %constant.134.clone.1..sunk) | dynamic-update-slice | bytes 1048580 | tf_op jit(solution)/shard_map/jvp()/while/body/jit(dynamic_update_index_in_dim)/dynamic_update_slice | solution.py:49
  99.1 3.5 fusion.231
  104.8 12.3 %dynamic_update_slice.68 = f32[4,256,8,64]{1,0,3,2:T(4,128)} dynamic-update-slice(f32[4,256,8,64]{1,0,3,2:T(4,128)} %get-tuple-element.828, f32[1,256,8,64]{1,0,3,2:T(1,128)S(1)} %copy.123, s32[]{:T(128)} %get-tuple-element.826, s32[]{:T(128)} %constant.134.clone.1..sunk, s32[]{:T(128)} %constant.134.clone.1..sunk, s32[]{:T(128)} %constant.134.clone.1..sunk) | dynamic-update-slice | bytes 1048580 | tf_op jit(solution)/shard_map/jvp()/while/body/jit(dynamic_update_index_in_dim)/dynamic_update_slice | solution.py:49
  122.1 3.5 fusion.231
  127.9 12.3 %dynamic_update_slice.68 = f32[4,256,8,64]{1,0,3,2:T(4,128)} dynamic-update-slice(f32[4,256,8,64]{1,0,3,2:T(4,128)} %get-tuple-element.828, f32[1,256,8,64]{1,0,3,2:T(1,128)S(1)} %copy.123, s32[]{:T(128)} %get-tuple-element.826, s32[]{:T(128)} %constant.134.clone.1..sunk, s32[]{:T(128)} %constant.134.clone.1..sunk, s32[]{:T(128)} %constant.134.clone.1..sunk) | dynamic-update-slice | bytes 1048580 | tf_op jit(solution)/shard_map/jvp()/while/body/jit(dynamic_update_index_in_dim)/dynamic_update_slice | solution.py:49
  145.2 3.5 fusion.231
  150.9 12.3 %dynamic_update_slice.68 = f32[4,256,8,64]{1,0,3,2:T(4,128)} dynamic-update-slice(f32[4,256,8,64]{1,0,3,2:T(4,128)} %get-tuple-element.828, f32[1,256,8,64]{1,0,3,2:T(1,128)S(1)} %copy.123, s32[]{:T(128)} %get-tuple-element.826, s32[]{:T(128)} %constant.134.clone.1..sunk, s32[]{:T(128)} %constant.134.clone.1..sunk, s32[]{:T(128)} %constant.134.clone.1..sunk) | dynamic-update-slice | bytes 1048580 | tf_op jit(solution)/shard_map/jvp()/while/body/jit(dynamic_update_index_in_dim)/dynamic_update_slice | solution.py:49
  169.3 6.0 %all-reduce.2 = (f32[1024]{0:T(1024)S(1)}, f32[1024]{0:T(1024)S(1)}) all-reduce(f32[1024]{0:T(1024)S(1)} %get-tuple-element.523, f32[1024]{0:T(1024)S(1)} %get-tuple-element.522), channel_id=1, replica_groups=mesh['dp'=4,'context'=8] {'dp'}, use_global_device_ids=true, to_apply=%region_10.11 | all-reduce | flops 2048 | bytes 16384 | tf_op jit(solution)/shard_map/psum | solution.py:102
  175.3 4.6 %fusion.99 = (bf16[1024,512]{0,1:T(8,128)(2,1)}, f32[1024,512]{0,1:T(8,128)S(1)}) fusion(bf16[1024,512]{0,1:T(8,128)(2,1)} %copy-done.2, f32[1024,512]{0,1:T(8,128)} %bitcast.347, bf16[1024,512]{0,1:T(8,128)(2,1)} %copy-done.1, f32[1024]{0:T(1024)S(1)} %get-tuple-element.597, f32[1024]{0:T(1024)S(1)} %get-tuple-element.596, f32[512]{0:T(512)S(1)} %copy-done.16), kind=kLoop, calls=%fused_computation.139 | loop fusion | flops 9961472 | bytes 7350272 | tf_op jit(solution)/shard_map/convert_element_type | solution.py:141
  184.1 45.7 %all-gather.8.cloned.1.call-done = f32[64,64,128]{2,1,0:T(8,128)} async-done(((f32[8,64,128]{2,1,0:T(8,128)}), f32[64,64,128]{2,1,0:T(8,128)}) %all-gather.8.cloned.1.call-update) | async-done | bytes 2097168 | tf_op jit(solution)/shard_map/all_gather | solution.py:121
  229.8 4.4 %fusion.100 = f32[8,1,64,128]{3,1,2,0:T(1,128)S(1)} fusion(f32[8,8,1,1]{0,2,3,1:T(1,128)S(1)} %copy.88, f32[8,8,64,128]{3,2,1,0:T(8,128)} %bitcast.350), kind=kOutput, calls=%fused_computation.140 | convolution fusion | flops 6291456 | bytes 2359552 | tf_op jit(solution)/shard_map/fh,fhpn->hpn/dot_general | solution.py:132
  237.7 127.6 %while.38 = (s32[]{:T(128)}, f32[8,64,128]{2,1,0:T(8,128)S(1)}, bf16[4,256,8,64]{1,3,2,0:T(8,128)(2,1)}, f32[4,256,128]{2,1,0:T(8,128)}, f32[4,256,128]{2,1,0:T(...) while((s32[]{:T(128)}, f32[8,64,128]{2,1,0:T(8,128)S(1)}, ...), condition=%wide.region_23.24_spmd, body=%wide.region_11.23_spmd.sunk | while | flops 2125232128 | bytes 24865956 | solution.py:49
  247.7 4.0 %fusion.215 = (f32[256,8]{0,1:T(8,128)}, f32[256,8]{0,1:T(8,128)}, f32[256,8]{0,1:T(8,128)}, f32[256,256]{1,0:T(8,128)S(1)}) fusion(f32[256,8]{0,1:T(8,128)S(1)} %get-tuple-element.788, f32[256,8]{0,1:T(8,128)S(1)} %get-tuple-element.783, f32[256,256]{1,0:T(8,128)S(1)} %fusion.214, pred[256,256]{1,0:T(8,128)(4,1)S(1)} %iota_compare_fusion.8, ...), kind=kOutput, calls=%fused_computation.66.clone.1 | convolution fusion | flops 409397248 | bytes 1679360 | tf_op jit(solution)/shard_map/transpose(jvp())/while/body/eval_jaxpr/checkpoint/tsh,shp->thp/dot_general | solution.py:27
  253.8 3.1 reduce-window.80
  279.6 4.0 %fusion.215 = (f32[256,8]{0,1:T(8,128)}, f32[256,8]{0,1:T(8,128)}, f32[256,8]{0,1:T(8,128)}, f32[256,256]{1,0:T(8,128)S(1)}) fusion(f32[256,8]{0,1:T(8,128)S(1)} %get-tuple-element.788, f32[256,8]{0,1:T(8,128)S(1)} %get-tuple-element.783, f32[256,256]{1,0:T(8,128)S(1)} %fusion.214, pred[256,256]{1,0:T(8,128)(4,1)S(1)} %iota_compare_fusion.8, ...), kind=kOutput, calls=%fused_computation.66.clone.1 | convolution fusion | flops 409397248 | bytes 1679360 | tf_op jit(solution)/shard_map/transpose(jvp())/while/body/eval_jaxpr/checkpoint/tsh,shp->thp/dot_general | solution.py:27
  285.7 3.1 reduce-window.80
  311.5 4.0 %fusion.215 = (f32[256,8]{0,1:T(8,128)}, f32[256,8]{0,1:T(8,128)}, f32[256,8]{0,1:T(8,128)}, f32[256,256]{1,0:T(8,128)S(1)}) fusion(f32[256,8]{0,1:T(8,128)S(1)} %get-tuple-element.788, f32[256,8]{0,1:T(8,128)S(1)} %get-tuple-element.783, f32[256,256]{1,0:T(8,128)S(1)} %fusion.214, pred[256,256]{1,0:T(8,128)(4,1)S(1)} %iota_compare_fusion.8, ...), kind=kOutput, calls=%fused_computation.66.clone.1 | convolution fusion | flops 409397248 | bytes 1679360 | tf_op jit(solution)/shard_map/transpose(jvp())/while/body/eval_jaxpr/checkpoint/tsh,shp->thp/dot_general | solution.py:27
  343.4 4.0 %fusion.215 = (f32[256,8]{0,1:T(8,128)}, f32[256,8]{0,1:T(8,128)}, f32[256,8]{0,1:T(8,128)}, f32[256,256]{1,0:T(8,128)S(1)}) fusion(f32[256,8]{0,1:T(8,128)S(1)} %get-tuple-element.788, f32[256,8]{0,1:T(8,128)S(1)} %get-tuple-element.783, f32[256,256]{1,0:T(8,128)S(1)} %fusion.214, pred[256,256]{1,0:T(8,128)(4,1)S(1)} %iota_compare_fusion.8, ...), kind=kOutput, calls=%fused_computation.66.clone.1 | convolution fusion | flops 409397248 | bytes 1679360 | tf_op jit(solution)/shard_map/transpose(jvp())/while/body/eval_jaxpr/checkpoint/tsh,shp->thp/dot_general | solution.py:27
  373.6 18.8 %reduce-scatter.2.cloned.1.call-done = f32[1024,64]{0,1:T(8,128)} async-done(((f32[1024,256]{0,1:T(8,128)}), f32[1024,64]{0,1:T(8,128)}) %reduce-scatter.2.cloned.1.call-update) | async-done | bytes 262160 | tf_op jit(solution)/shard_map/reduce_scatter | solution.py:138
  (311 shorter events, 170.1 us)
Async XLA Ops:
  7.2 62.2 %all-gather.6.cloned.1.call-start = ((), (), s32[]{:S(2)}) async-start(), calls=%async_computation.2 | async-start | bytes 2359296 | tf_op jit(solution)/shard_map/all_gather | solution.py:78
  17.3 212.5 %all-gather.8.cloned.1.call-start = ((), (), s32[]{:S(2)}) async-start(), calls=%async_computation.3 | async-start | bytes 2359296 | tf_op jit(solution)/shard_map/all_gather | solution.py:121
  45.0 123.0 %copy-start.1 = (bf16[1024,512]{0,1:T(8,128)(2,1)}, bf16[1024,512]{0,1:T(8,128)(2,1)S(1)}, u32[]{:S(2)}) copy-start(bf16[1024,512]{0,1:T(8,128)(2,1)S(1)} %copy.69) | copy-start | bytes 3145732
  45.0 28.8 %copy-start.7 = (f32[1024,8]{0,1:T(8,128)S(1)}, f32[1024,8]{0,1:T(8,128)}, u32[]{:S(2)}) copy-start(f32[1024,8]{0,1:T(8,128)} %param.17) | copy-start | bytes 98308
  46.9 121.1 %copy-start.2 = (bf16[1024,512]{0,1:T(8,128)(2,1)}, bf16[1024,512]{0,1:T(8,128)(2,1)S(1)}, u32[]{:S(2)}) copy-start(bf16[1024,512]{0,1:T(8,128)(2,1)S(1)} %copy.73) | copy-start | bytes 3145732
  175.3 4.6 %copy-start.11 = (bf16[1024,128]{1,0:T(8,128)(2,1)S(1)}, bf16[1024,128]{1,0:T(8,128)(2,1)}, u32[]{:S(2)}) copy-start(bf16[1024,128]{1,0:T(8,128)(2,1)} %param.16) | copy-start | bytes 786436
  181.8 210.6 %reduce-scatter.2.cloned.1.call-start = ((), (), s32[]{:S(2)}) async-start(), calls=%async_computation.1 | async-start | bytes 1310720 | tf_op jit(solution)/shard_map/reduce_scatter | solution.py:138
  247.6 4.1 %copy-start.14 = (f32[256,8]{0,1:T(8,128)}, f32[256,8]{0,1:T(8,128)S(1)}, u32[]{:S(2)}) copy-start(f32[256,8]{0,1:T(8,128)S(1)} %get-tuple-element.788) | copy-start | bytes 24580 | tf_op jit(solution)/shard_map/transpose(jvp())/while
  258.8 6.4 %copy-start.4 = (bf16[4,256,8,64]{1,3,2,0:T(8,128)(2,1)S(1)}, bf16[4,256,8,64]{1,3,2,0:T(8,128)(2,1)}, u32[]{:S(2)}) copy-start(bf16[4,256,8,64]{1,3,2,0:T(8,128)(2,1)} %get-tuple-element.873) | copy-start | bytes 3145732 | tf_op jit(solution)/shard_map/transpose(jvp())/while
  258.8 6.4 %copy-start.15 = (f32[256,8]{0,1:T(8,128)S(1)}, f32[256,8]{0,1:T(8,128)}, u32[]{:S(2)}) copy-start(f32[256,8]{0,1:T(8,128)} %copy-done.14) | copy-start | bytes 24580 | tf_op jit(solution)/shard_map/transpose(jvp())/while
  265.3 3.6 copy-start.13
  279.5 4.1 %copy-start.14 = (f32[256,8]{0,1:T(8,128)}, f32[256,8]{0,1:T(8,128)S(1)}, u32[]{:S(2)}) copy-start(f32[256,8]{0,1:T(8,128)S(1)} %get-tuple-element.788) | copy-start | bytes 24580 | tf_op jit(solution)/shard_map/transpose(jvp())/while
  290.7 6.5 %copy-start.4 = (bf16[4,256,8,64]{1,3,2,0:T(8,128)(2,1)S(1)}, bf16[4,256,8,64]{1,3,2,0:T(8,128)(2,1)}, u32[]{:S(2)}) copy-start(bf16[4,256,8,64]{1,3,2,0:T(8,128)(2,1)} %get-tuple-element.873) | copy-start | bytes 3145732 | tf_op jit(solution)/shard_map/transpose(jvp())/while
  290.7 6.5 %copy-start.15 = (f32[256,8]{0,1:T(8,128)S(1)}, f32[256,8]{0,1:T(8,128)}, u32[]{:S(2)}) copy-start(f32[256,8]{0,1:T(8,128)} %copy-done.14) | copy-start | bytes 24580 | tf_op jit(solution)/shard_map/transpose(jvp())/while
  297.2 3.6 copy-start.13
  311.5 4.1 %copy-start.14 = (f32[256,8]{0,1:T(8,128)}, f32[256,8]{0,1:T(8,128)S(1)}, u32[]{:S(2)}) copy-start(f32[256,8]{0,1:T(8,128)S(1)} %get-tuple-element.788) | copy-start | bytes 24580 | tf_op jit(solution)/shard_map/transpose(jvp())/while
  322.7 6.4 %copy-start.4 = (bf16[4,256,8,64]{1,3,2,0:T(8,128)(2,1)S(1)}, bf16[4,256,8,64]{1,3,2,0:T(8,128)(2,1)}, u32[]{:S(2)}) copy-start(bf16[4,256,8,64]{1,3,2,0:T(8,128)(2,1)} %get-tuple-element.873) | copy-start | bytes 3145732 | tf_op jit(solution)/shard_map/transpose(jvp())/while
  322.7 6.4 %copy-start.15 = (f32[256,8]{0,1:T(8,128)S(1)}, f32[256,8]{0,1:T(8,128)}, u32[]{:S(2)}) copy-start(f32[256,8]{0,1:T(8,128)} %copy-done.14) | copy-start | bytes 24580 | tf_op jit(solution)/shard_map/transpose(jvp())/while
  329.1 3.6 copy-start.13
  343.4 4.1 %copy-start.14 = (f32[256,8]{0,1:T(8,128)}, f32[256,8]{0,1:T(8,128)S(1)}, u32[]{:S(2)}) copy-start(f32[256,8]{0,1:T(8,128)S(1)} %get-tuple-element.788) | copy-start | bytes 24580 | tf_op jit(solution)/shard_map/transpose(jvp())/while
  354.6 6.4 %copy-start.4 = (bf16[4,256,8,64]{1,3,2,0:T(8,128)(2,1)S(1)}, bf16[4,256,8,64]{1,3,2,0:T(8,128)(2,1)}, u32[]{:S(2)}) copy-start(bf16[4,256,8,64]{1,3,2,0:T(8,128)(2,1)} %get-tuple-element.873) | copy-start | bytes 3145732 | tf_op jit(solution)/shard_map/transpose(jvp())/while
  354.6 6.4 %copy-start.15 = (f32[256,8]{0,1:T(8,128)S(1)}, f32[256,8]{0,1:T(8,128)}, u32[]{:S(2)}) copy-start(f32[256,8]{0,1:T(8,128)} %copy-done.14) | copy-start | bytes 24580 | tf_op jit(solution)/shard_map/transpose(jvp())/while
  361.0 3.6 copy-start.13
  366.5 2.4 copy-start.3
  (14 other events, 15.1 us)
Sparse Core Ops, SparseCore 0:
  17.4 51.8 all-gather.5
  181.9 47.9 all-gather.7
  369.1 23.2 reduce-scatter.1
where the time goes:
time: 402 us; the launch traced here: 399 us
  local copies, waits for them, and re-layouts  115 us (29%)
  matrix products  98.3 us (24%)
  waiting for transfers between devices  86.3 us (21%)
  other arithmetic  56.4 us (14%)
  blocking collectives  28.5 us (7%)
  between operations  14 us (3%)
    dynamic_update_slice x12, local copies, waits for them, and re-layouts, recurrence(): end_state, outputs = lax.scan(advance, start_state, pieces)  54.4 us
    all_gather x1, waiting for transfers between devices, on_device(): pieces = lax.all_gather(influence[None], 'context', axis=0, tiled=True)  45.7 us
    dot_general x12, matrix products, block_step(): within = jnp.einsum('tsh,shp->thp', mixing, signal_block, precision=highest)  40.6 us
    another operation x40, other arithmetic  34.5 us
    all_gather x1, blocking collectives, on_device(): all_totals = lax.all_gather(totals[None, :], 'context', axis=0, tiled=True)  22.6 us
    all_gather x1, waiting for transfers between devices, on_device(): pieces = lax.all_gather(local_end[None], 'context', axis=0, tiled=True)  21.7 us
    reduce_scatter x1, waiting for transfers between devices, on_device(): lax.psum_scatter(jnp.concatenate([grad_writer, grad_reader], axis=1), 'dp...  18.8 us
    dot_general x16, matrix products, block_step(): jnp.dot(reader_block, writer_block.T, precision=highest, preferred_elemen...  15.9 us
  transfers between devices with their start and end apart: 3, of which 3 were waited for; matrix products, arithmetic and copies ran while one was open for 3% of the time, Pallas kernels for 0%

commit v1 on v0

--- a/solution.py
+++ b/solution.py
@@ -9,6 +9,28 @@
 SPAN = 256
 highest = lax.Precision.HIGHEST
 epsilon = 1e-05
+
+
+def in_order(blocks, dim):
+    shape = list(blocks.shape[1:])
+    shape[dim] *= blocks.shape[0]
+    return jnp.moveaxis(blocks, 0, dim).reshape(shape)
+
+
+def gather_around(shard, axis, dim):
+    count = lax.axis_size(axis)
+    pairs = [(i, (i + 1) % count) for i in range(count)]
+    back = [(b, a) for a, b in pairs]
+    lower, upper = ([], [])
+    for lap in range(count - 1):
+        if lap % 2 == 0:
+            lower.append(lax.ppermute(lower[-1] if lower else shard, axis, pairs))
+        else:
+            upper.append(lax.ppermute(upper[-1] if upper else shard, axis, back))
+    parts = jnp.stack([*lower[::-1], shard, *upper])
+    shift = lax.axis_index(axis) - len(lower)
+    parts = parts[(jnp.arange(count) - shift) % count]
+    return in_order(parts, dim)
 
 
 def block_step(state, pieces, decay_rate, skip_gain):
@@ -75,7 +97,7 @@
     mine = (jnp.arange(devices) == position).astype(jnp.float32)
     inclusive_mine = jnp.dot(mine, inclusive, precision=highest, preferred_element_type=jnp.float32)
     exclusive_mine = jnp.dot(mine, exclusive, precision=highest, preferred_element_type=jnp.float32)
-    pieces = lax.all_gather(local_end[None], "context", axis=0, tiled=True)
+    pieces = gather_around(local_end[None], "context", 0)
     indices = jnp.arange(pieces.shape[0])
     select = (indices[:, None] == jnp.arange(devices)[None, :]).astype(jnp.float32)
     inclusive_from = jnp.dot(

time: 402 us -> 418 us (1.040)
  starting transfers between devices: 0.12 us -> 15.4 us
  local copies, waits for them, and re-layouts: 115 us -> 127 us
  waiting for transfers between devices: 86.3 us -> 78.7 us
    all_gather x1 -> x0, waiting for transfers between devices: 21.7 us -> none  [on_device(): pieces = lax.all_gather(local_end[None], 'context', axis=0, tiled=True)]
    ppermute x0 -> x7, waiting for transfers between devices: none -> 15.5 us  [the longest x4 15.5 us: gather_around(): lower.append(lax.ppermute(lower[-1] if lower else shard, axis, pairs))]
    ppermute x0 -> x7, starting transfers between devices: none -> 15.3 us  [the longest x3 8.02 us: gather_around(): upper.append(lax.ppermute(upper[-1] if upper else shard, axis, back))]
    unnamed x31 -> x50, local copies, waits for them, and re-layouts: 13.8 us -> 22.7 us
    another operation x29 -> x30, local copies, waits for them, and re-layouts: 9.94 us -> 10.7 us
  transfers between devices with their start and end apart: 3 -> 9, of which waited for: 3 -> 4; matrix products, arithmetic and copies ran while one was open for 3% -> 6% of each run, Pallas kernels for 0% -> 0%
where the time goes in v1:
time: 418 us; the launch traced here: 415 us
  local copies, waits for them, and re-layouts  127 us (30%)
  matrix products  97.4 us (23%)
  waiting for transfers between devices  78.7 us (19%)
  other arithmetic  56.4 us (13%)
  blocking collectives  24.5 us (6%)
  starting transfers between devices  15.4 us (4%)
  between operations  14.4 us (3%)
    dynamic_update_slice x12, local copies, waits for them, and re-layouts, recurrence(): end_state, outputs = lax.scan(advance, start_state, pieces)  54.4 us
    all_gather x1, waiting for transfers between devices, on_device(): pieces = lax.all_gather(influence[None], 'context', axis=0, tiled=True)  44.3 us
    dot_general x12, matrix products, block_step(): within = jnp.einsum('tsh,shp->thp', mixing, signal_block, precision=highest)  40.5 us
    another operation x40, other arithmetic  34.5 us
    unnamed x50, local copies, waits for them, and re-layouts  22.7 us
    reduce_scatter x1, waiting for transfers between devices, on_device(): lax.psum_scatter(jnp.concatenate([grad_writer, grad_reader], axis=1), 'dp...  18.8 us
    all_gather x1, blocking collectives, on_device(): all_totals = lax.all_gather(totals[None, :], 'context', axis=0, tiled=True)  18.5 us
    dot_general x16, matrix products, block_step(): jnp.dot(reader_block, writer_block.T, precision=highest, preferred_elemen...  15.8 us
  transfers between devices with their start and end apart: 9, of which 4 were waited for; matrix products, arithmetic and copies ran while one was open for 6% of the time, Pallas kernels for 0%

profile of v1, /device:TPU:0, one launch (start us, length us, event | category | flops | bytes accessed | tf_op | source)
XLA Modules:
  0.0 414.9 jit_solution(5489252964611087798)
XLA Ops:
  19.6 9.3 %collective-permute-done = f32[1,8,64,128]{3,2,1,0:T(8,128)S(1)} collective-permute-done((f32[1,8,64,128]{3,2,1,0:T(8,128)S(1)}, f32[1,8,64,128]{3,2,1,0:T(8,128)S(1)}, u32[]{:S(2)}, u32[]{:S(2)}) %collective-permute-start) | collective-permute-done | bytes 262176 | tf_op jit(solution)/shard_map/ppermute | solution.py:27
  29.0 4.7 %collective-permute-start.4 = (f32[1,8,64,128]{3,2,1,0:T(8,128)S(1)}, f32[1,8,64,128]{3,2,1,0:T(8,128)}, u32[]{:S(2)}, u32[]{:S(2)}) collective-permute-start(f32[1,8,64,128]{3,2,1,0:T(8,128)S(1)} %bitcast.376), channel_id=1, source_target_pairs={{1,0},{2,1},{3,2},{4,3},{5,4},{6,5},{7,6},{0,7},{9,8},{10,9},{11,1... | collective-permute-start | bytes 786440 | tf_op jit(solution)/shard_map/ppermute | solution.py:29
  33.7 6.2 %collective-permute-done.1 = f32[1,8,64,128]{3,2,1,0:T(8,128)S(1)} collective-permute-done((f32[1,8,64,128]{3,2,1,0:T(8,128)S(1)}, f32[1,8,64,128]{3,2,1,0:T(8,128)S(1)}, u32[]{:S(2)}, u32[]{:S(2)}) %collective-permute-start.1) | collective-permute-done | bytes 262176 | tf_op jit(solution)/shard_map/ppermute | solution.py:27
  42.3 18.5 %all-gather.1 = f32[8,1,8]{2,1,0:T(1,128)S(1)} all-gather(f32[1,1,8]{2,1,0:T(1,128)S(1)} %bitcast.386), channel_id=1, replica_groups=mesh['dp'=4,'context'=8] {'context'}, dimensions={0}, use_global_device_ids=true | all-gather | bytes 288 | tf_op jit(solution)/shard_map/all_gather | solution.py:92
  83.3 3.6 gather_fusion
  86.9 4.4 %fusion.102 = f32[8,1,64,128]{3,1,2,0:T(1,128)S(1)} fusion(f32[8,8,1,1]{0,2,3,1:T(1,128)S(1)} %copy.85, f32[8,8,64,128]{3,2,1,0:T(8,128)} %gather_fusion), kind=kOutput, calls=%fused_computation.143 | convolution fusion | flops 6291456 | bytes 2359552 | tf_op jit(solution)/shard_map/fh,fhpn->hpn/dot_general | solution.py:111
  91.3 92.1 %while.39 = (s32[]{:T(128)}, f32[8,64,128]{2,1,0:T(8,128)S(1)}, f32[4,256,8,64]{1,0,3,2:T(4,128)}, f32[4,8,64,128]{3,2,1,0:T(8,128)}, f32[4,256,8]{1,2,0:T(8,128...) while((s32[]{:T(128)}, f32[8,64,128]{2,1,0:T(8,128)S(1)}, ...), condition=%wide.region_6.7_spmd.clone, body=%wide.region_3.6_spmd.clone.sunk | while | flops 909158400 | bytes 7812925 | solution.py:71
  99.3 12.3 %dynamic_update_slice.68 = f32[4,256,8,64]{1,0,3,2:T(4,128)} dynamic-update-slice(f32[4,256,8,64]{1,0,3,2:T(4,128)} %get-tuple-element.828, f32[1,256,8,64]{1,0,3,2:T(1,128)S(1)} %copy.123, s32[]{:T(128)} %get-tuple-element.826, s32[]{:T(128)} %constant.150.clone.1..sunk, s32[]{:T(128)} %constant.150.clone.1..sunk, s32[]{:T(128)} %constant.150.clone.1..sunk) | dynamic-update-slice | bytes 1048580 | tf_op jit(solution)/shard_map/jvp()/while/body/jit(dynamic_update_index_in_dim)/dynamic_update_slice | solution.py:71
  116.6 3.5 fusion.233
  122.4 12.3 %dynamic_update_slice.68 = f32[4,256,8,64]{1,0,3,2:T(4,128)} dynamic-update-slice(f32[4,256,8,64]{1,0,3,2:T(4,128)} %get-tuple-element.828, f32[1,256,8,64]{1,0,3,2:T(1,128)S(1)} %copy.123, s32[]{:T(128)} %get-tuple-element.826, s32[]{:T(128)} %constant.150.clone.1..sunk, s32[]{:T(128)} %constant.150.clone.1..sunk, s32[]{:T(128)} %constant.150.clone.1..sunk) | dynamic-update-slice | bytes 1048580 | tf_op jit(solution)/shard_map/jvp()/while/body/jit(dynamic_update_index_in_dim)/dynamic_update_slice | solution.py:71
  139.6 3.5 fusion.233
  145.4 12.3 %dynamic_update_slice.68 = f32[4,256,8,64]{1,0,3,2:T(4,128)} dynamic-update-slice(f32[4,256,8,64]{1,0,3,2:T(4,128)} %get-tuple-element.828, f32[1,256,8,64]{1,0,3,2:T(1,128)S(1)} %copy.123, s32[]{:T(128)} %get-tuple-element.826, s32[]{:T(128)} %constant.150.clone.1..sunk, s32[]{:T(128)} %constant.150.clone.1..sunk, s32[]{:T(128)} %constant.150.clone.1..sunk) | dynamic-update-slice | bytes 1048580 | tf_op jit(solution)/shard_map/jvp()/while/body/jit(dynamic_update_index_in_dim)/dynamic_update_slice | solution.py:71
  162.7 3.5 fusion.233
  168.4 12.3 %dynamic_update_slice.68 = f32[4,256,8,64]{1,0,3,2:T(4,128)} dynamic-update-slice(f32[4,256,8,64]{1,0,3,2:T(4,128)} %get-tuple-element.828, f32[1,256,8,64]{1,0,3,2:T(1,128)S(1)} %copy.123, s32[]{:T(128)} %get-tuple-element.826, s32[]{:T(128)} %constant.150.clone.1..sunk, s32[]{:T(128)} %constant.150.clone.1..sunk, s32[]{:T(128)} %constant.150.clone.1..sunk) | dynamic-update-slice | bytes 1048580 | tf_op jit(solution)/shard_map/jvp()/while/body/jit(dynamic_update_index_in_dim)/dynamic_update_slice | solution.py:71
  186.8 6.0 %all-reduce.2 = (f32[1024]{0:T(1024)S(1)}, f32[1024]{0:T(1024)S(1)}) all-reduce(f32[1024]{0:T(1024)S(1)} %get-tuple-element.523, f32[1024]{0:T(1024)S(1)} %get-tuple-element.522), channel_id=1, replica_groups=mesh['dp'=4,'context'=8] {'dp'}, use_global_device_ids=true, to_apply=%region_10.11 | all-reduce | flops 2048 | bytes 16384 | tf_op jit(solution)/shard_map/psum | solution.py:124
  192.8 4.6 %fusion.99 = (bf16[1024,512]{0,1:T(8,128)(2,1)}, f32[1024,512]{0,1:T(8,128)S(1)}) fusion(bf16[1024,512]{0,1:T(8,128)(2,1)} %copy-done.2, f32[1024,512]{0,1:T(8,128)} %bitcast.366, bf16[1024,512]{0,1:T(8,128)(2,1)} %copy-done.1, f32[1024]{0:T(1024)S(1)} %get-tuple-element.597, f32[1024]{0:T(1024)S(1)} %get-tuple-element.596, f32[512]{0:T(512)S(1)} %copy-done.22), kind=kLoop, calls=%fused_computation.140 | loop fusion | flops 9961472 | bytes 7350272 | tf_op jit(solution)/shard_map/convert_element_type | solution.py:163
  201.7 44.3 %all-gather.4.cloned.1.call-done = f32[64,64,128]{2,1,0:T(8,128)} async-done(((f32[8,64,128]{2,1,0:T(8,128)}), f32[64,64,128]{2,1,0:T(8,128)}) %all-gather.4.cloned.1.call-update) | async-done | bytes 2097168 | tf_op jit(solution)/shard_map/all_gather | solution.py:143
  246.0 4.4 %fusion.100 = f32[8,1,64,128]{3,1,2,0:T(1,128)S(1)} fusion(f32[8,8,1,1]{0,2,3,1:T(1,128)S(1)} %copy.88, f32[8,8,64,128]{3,2,1,0:T(8,128)} %bitcast.368), kind=kOutput, calls=%fused_computation.141 | convolution fusion | flops 6291456 | bytes 2359552 | tf_op jit(solution)/shard_map/fh,fhpn->hpn/dot_general | solution.py:154
  253.8 127.1 %while.38 = (s32[]{:T(128)}, f32[8,64,128]{2,1,0:T(8,128)S(1)}, bf16[4,256,8,64]{1,3,2,0:T(8,128)(2,1)}, f32[4,256,128]{2,1,0:T(8,128)}, f32[4,256,128]{2,1,0:T(...) while((s32[]{:T(128)}, f32[8,64,128]{2,1,0:T(8,128)S(1)}, ...), condition=%wide.region_23.24_spmd, body=%wide.region_11.23_spmd.sunk | while | flops 2125232128 | bytes 24865956 | solution.py:71
  263.7 4.0 fusion.217
  295.5 4.0 fusion.217
  327.3 4.0 fusion.217
  359.1 4.0 fusion.217
  389.2 18.8 %reduce-scatter.2.cloned.1.call-done = f32[1024,64]{0,1:T(8,128)} async-done(((f32[1024,256]{0,1:T(8,128)}), f32[1024,64]{0,1:T(8,128)}) %reduce-scatter.2.cloned.1.call-update) | async-done | bytes 262160 | tf_op jit(solution)/shard_map/reduce_scatter | solution.py:160
  (345 shorter events, 199.1 us)
Async XLA Ops:
  7.2 238.8 %all-gather.4.cloned.1.call-start = ((), (), s32[]{:S(2)}) async-start(), calls=%async_computation.2 | async-start | bytes 2359296 | tf_op jit(solution)/shard_map/all_gather | solution.py:143
  16.6 46.7 %copy-start.12 = (f32[8,64,128]{2,1,0:T(8,128)}, f32[8,64,128]{2,1,0:T(8,128)S(1)}, u32[]{:S(2)}) copy-start(f32[8,64,128]{2,1,0:T(8,128)S(1)} %fusion.106) | copy-start | bytes 786436
  16.6 12.4 %collective-permute-start = (f32[1,8,64,128]{3,2,1,0:T(8,128)S(1)}, f32[1,8,64,128]{3,2,1,0:T(8,128)S(1)}, u32[]{:S(2)}, u32[]{:S(2)}) collective-permute-start(f32[1,8,64,128]{3,2,1,0:T(8,128)S(1)} %bitcast.375), channel_id=1, source_target_pairs={{0,1},{1,2},{2,3},{3,4},{4,5},{5,6},{6,7},{7,0},{8,9},{9,10},{10,1... | collective-permute-start | bytes 786440 | tf_op jit(solution)/shard_map/ppermute | solution.py:27
  29.0 34.3 %copy-start.14 = (f32[1,8,64,128]{3,2,1,0:T(8,128)}, f32[1,8,64,128]{3,2,1,0:T(8,128)S(1)}, u32[]{:S(2)}) copy-start(f32[1,8,64,128]{3,2,1,0:T(8,128)S(1)} %collective-permute-done) | copy-start | bytes 786436
  29.0 10.9 %collective-permute-start.1 = (f32[1,8,64,128]{3,2,1,0:T(8,128)S(1)}, f32[1,8,64,128]{3,2,1,0:T(8,128)S(1)}, u32[]{:S(2)}, u32[]{:S(2)}) collective-permute-start(f32[1,8,64,128]{3,2,1,0:T(8,128)S(1)} %collective-permute-done), channel_id=1, source_target_pairs={{0,1},{1,2},{2,3},{3,4},{4,5},{5,6},{6,7},{7,0},{8,9},{9,10},{10,1... | collective-permute-start | bytes 786440 | tf_op jit(solution)/shard_map/ppermute | solution.py:27
  29.0 32.2 %collective-permute-start.4 = (f32[1,8,64,128]{3,2,1,0:T(8,128)S(1)}, f32[1,8,64,128]{3,2,1,0:T(8,128)}, u32[]{:S(2)}, u32[]{:S(2)}) collective-permute-start(f32[1,8,64,128]{3,2,1,0:T(8,128)S(1)} %bitcast.376), channel_id=1, source_target_pairs={{1,0},{2,1},{3,2},{4,3},{5,4},{6,5},{7,6},{0,7},{9,8},{10,9},{11,1... | collective-permute-start | bytes 786440 | tf_op jit(solution)/shard_map/ppermute | solution.py:29
  39.9 23.4 %copy-start.16 = (f32[1,8,64,128]{3,2,1,0:T(8,128)}, f32[1,8,64,128]{3,2,1,0:T(8,128)S(1)}, u32[]{:S(2)}) copy-start(f32[1,8,64,128]{3,2,1,0:T(8,128)S(1)} %collective-permute-done.1) | copy-start | bytes 786436
  39.9 21.6 %collective-permute-start.2 = (f32[1,8,64,128]{3,2,1,0:T(8,128)S(1)}, f32[1,8,64,128]{3,2,1,0:T(8,128)}, u32[]{:S(2)}, u32[]{:S(2)}) collective-permute-start(f32[1,8,64,128]{3,2,1,0:T(8,128)S(1)} %collective-permute-done.1), channel_id=1, source_target_pairs={{0,1},{1,2},{2,3},{3,4},{4,5},{5,6},{6,7},{7,0},{8,9},{9,10},{10,1... | collective-permute-start | bytes 786440 | tf_op jit(solution)/shard_map/ppermute | solution.py:27
  61.1 9.5 %collective-permute-start.5 = (f32[1,8,64,128]{3,2,1,0:T(8,128)}, f32[1,8,64,128]{3,2,1,0:T(8,128)}, u32[]{:S(2)}, u32[]{:S(2)}) collective-permute-start(f32[1,8,64,128]{3,2,1,0:T(8,128)} %collective-permute-done.4), channel_id=1, source_target_pairs={{1,0},{2,1},{3,2},{4,3},{5,4},{6,5},{7,6},{0,7},{9,8},{10,9},{11,1... | collective-permute-start | bytes 786440 | tf_op jit(solution)/shard_map/ppermute | solution.py:29
  61.5 12.2 %collective-permute-start.3 = (f32[1,8,64,128]{3,2,1,0:T(8,128)}, f32[1,8,64,128]{3,2,1,0:T(8,128)}, u32[]{:S(2)}, u32[]{:S(2)}) collective-permute-start(f32[1,8,64,128]{3,2,1,0:T(8,128)} %collective-permute-done.2), channel_id=1, source_target_pairs={{0,1},{1,2},{2,3},{3,4},{4,5},{5,6},{6,7},{7,0},{8,9},{9,10},{10,1... | collective-permute-start | bytes 786440 | tf_op jit(solution)/shard_map/ppermute | solution.py:27
  68.0 117.6 %copy-start.1 = (bf16[1024,512]{0,1:T(8,128)(2,1)}, bf16[1024,512]{0,1:T(8,128)(2,1)S(1)}, u32[]{:S(2)}) copy-start(bf16[1024,512]{0,1:T(8,128)(2,1)S(1)} %copy.69) | copy-start | bytes 3145732
  68.0 9.0 %copy-start.17 = (f32[1,8,64,128]{3,2,1,0:T(8,128)S(1)}, f32[1,8,64,128]{3,2,1,0:T(8,128)}, u32[]{:S(2)}) copy-start(f32[1,8,64,128]{3,2,1,0:T(8,128)} %copy-done.16) | copy-start | bytes 786436
  68.0 9.7 %copy-start.15 = (f32[1,8,64,128]{3,2,1,0:T(8,128)S(1)}, f32[1,8,64,128]{3,2,1,0:T(8,128)}, u32[]{:S(2)}) copy-start(f32[1,8,64,128]{3,2,1,0:T(8,128)} %copy-done.14) | copy-start | bytes 786436
  68.0 10.4 %copy-start.13 = (f32[8,64,128]{2,1,0:T(8,128)S(1)}, f32[8,64,128]{2,1,0:T(8,128)}, u32[]{:S(2)}) copy-start(f32[8,64,128]{2,1,0:T(8,128)} %copy-done.12) | copy-start | bytes 786436
  69.9 115.6 %copy-start.2 = (bf16[1024,512]{0,1:T(8,128)(2,1)}, bf16[1024,512]{0,1:T(8,128)(2,1)S(1)}, u32[]{:S(2)}) copy-start(bf16[1024,512]{0,1:T(8,128)(2,1)S(1)} %copy.73) | copy-start | bytes 3145732
  70.7 11.9 %collective-permute-start.6 = (f32[1,8,64,128]{3,2,1,0:T(8,128)}, f32[1,8,64,128]{3,2,1,0:T(8,128)S(1)}, u32[]{:S(2)}, u32[]{:S(2)}) collective-permute-start(f32[1,8,64,128]{3,2,1,0:T(8,128)} %collective-permute-done.5), channel_id=1, source_target_pairs={{1,0},{2,1},{3,2},{4,3},{5,4},{6,5},{7,6},{0,7},{9,8},{10,9},{11,1... | collective-permute-start | bytes 786440 | tf_op jit(solution)/shard_map/ppermute | solution.py:29
  199.3 208.8 %reduce-scatter.2.cloned.1.call-start = ((), (), s32[]{:S(2)}) async-start(), calls=%async_computation.1 | async-start | bytes 1310720 | tf_op jit(solution)/shard_map/reduce_scatter | solution.py:160
  274.9 6.4 %copy-start.4 = (bf16[4,256,8,64]{1,3,2,0:T(8,128)(2,1)S(1)}, bf16[4,256,8,64]{1,3,2,0:T(8,128)(2,1)}, u32[]{:S(2)}) copy-start(bf16[4,256,8,64]{1,3,2,0:T(8,128)(2,1)} %get-tuple-element.873) | copy-start | bytes 3145732 | tf_op jit(solution)/shard_map/transpose(jvp())/while
  274.9 6.4 %copy-start.21 = (f32[256,8]{0,1:T(8,128)S(1)}, f32[256,8]{0,1:T(8,128)}, u32[]{:S(2)}) copy-start(f32[256,8]{0,1:T(8,128)} %copy-done.20) | copy-start | bytes 24580 | tf_op jit(solution)/shard_map/transpose(jvp())/while
  306.7 6.5 %copy-start.4 = (bf16[4,256,8,64]{1,3,2,0:T(8,128)(2,1)S(1)}, bf16[4,256,8,64]{1,3,2,0:T(8,128)(2,1)}, u32[]{:S(2)}) copy-start(bf16[4,256,8,64]{1,3,2,0:T(8,128)(2,1)} %get-tuple-element.873) | copy-start | bytes 3145732 | tf_op jit(solution)/shard_map/transpose(jvp())/while
  306.7 6.5 %copy-start.21 = (f32[256,8]{0,1:T(8,128)S(1)}, f32[256,8]{0,1:T(8,128)}, u32[]{:S(2)}) copy-start(f32[256,8]{0,1:T(8,128)} %copy-done.20) | copy-start | bytes 24580 | tf_op jit(solution)/shard_map/transpose(jvp())/while
  338.5 6.4 %copy-start.4 = (bf16[4,256,8,64]{1,3,2,0:T(8,128)(2,1)S(1)}, bf16[4,256,8,64]{1,3,2,0:T(8,128)(2,1)}, u32[]{:S(2)}) copy-start(bf16[4,256,8,64]{1,3,2,0:T(8,128)(2,1)} %get-tuple-element.873) | copy-start | bytes 3145732 | tf_op jit(solution)/shard_map/transpose(jvp())/while
  338.5 6.4 %copy-start.21 = (f32[256,8]{0,1:T(8,128)S(1)}, f32[256,8]{0,1:T(8,128)}, u32[]{:S(2)}) copy-start(f32[256,8]{0,1:T(8,128)} %copy-done.20) | copy-start | bytes 24580 | tf_op jit(solution)/shard_map/transpose(jvp())/while
  370.2 6.4 %copy-start.21 = (f32[256,8]{0,1:T(8,128)S(1)}, f32[256,8]{0,1:T(8,128)}, u32[]{:S(2)}) copy-start(f32[256,8]{0,1:T(8,128)} %copy-done.20) | copy-start | bytes 24580 | tf_op jit(solution)/shard_map/transpose(jvp())/while
  (26 other events, 63.1 us)
Sparse Core Ops, SparseCore 0:
  199.4 46.5 all-gather.3
  384.7 23.2 reduce-scatter.1
